TPU v7x, 256 devices: a whole 4x4x8 slice. The times are simulated.
256 devices in a mesh: gx: 16 (over x, z_hi), gy: 16 (over z_lo, y, core).
Axes of the slice: x: 4, y: 4, z: 8 (z_hi: 4, z_lo: 2; z = z_hi * 2 + z_lo), core: 2. Of those that a mesh axis runs over, the one named last changes fastest.
Arguments:
- tokens: bfloat16 [256, 256, 2, 512], P('gx', 'gy'), may hold values from -6 to 6
- cotangent: bfloat16 [256, 256, 2, 512], P('gx', 'gy'), may hold values from -6 to 6
- gain_x: float32 [512], replicated, may hold values from 0.1 to 1.9
- w_qkv_x: bfloat16 [512, 1536], replicated, may hold values from -5 to 5, as said below
- w_out_x: bfloat16 [512, 512], replicated, may hold values from -0.25 to 0.25
- gain_y: float32 [512], replicated, may hold values from 0.1 to 1.9
- w_qkv_y: bfloat16 [512, 1536], replicated, may hold values from -5 to 5, as said below
- w_out_y: bfloat16 [512, 512], replicated, may hold values from -0.25 to 0.25
- gain_mlp: float32 [512], replicated, may hold values from 0.1 to 1.9
- w_up: bfloat16 [512, 2048], replicated, may hold values from -0.25 to 0.25
- w_down: bfloat16 [2048, 512], replicated, may hold values from -0.125 to 0.125
Outputs:
- grad_tokens: bfloat16 [256, 256, 2, 512], P('gx', 'gy')
Inputs may be any that keep to these rules, and one draw needn't show every extreme that they name: `w_qkv_x`: query, key and value projections side by side. `w_qkv_y`: query, key and value projections side by side.
All inputs are finite; a program needn't handle non-finite values.
Results may differ from a plain program's by a relative error of at most 0.013.
Values may be sent and summed in bfloat16 or wider, within the bound.
A program may use at most 128 MiB of HBM per device.

v0:
```python
from functools import partial
import jax
import jax.numpy as jnp
from jax import lax
from jax.sharding import PartitionSpec as P

D = 512
HEADS = 8


def to_low(tensor):
    return lax.optimization_barrier(tensor.astype(jnp.bfloat16))


def layer_norm(inputs, norm_gain):
    average = jnp.mean(inputs, -1, keepdims=True)
    centred = inputs - average
    variance = jnp.mean(centred * centred, -1, keepdims=True)
    return centred * lax.rsqrt(variance + 1e-05) * norm_gain


def norm_back(inputs, norm_gain, gradient):
    _, pullback = jax.vjp(lambda tensor: layer_norm(tensor, norm_gain), inputs)
    return pullback(gradient)[0]


def project(tensor, weight):
    lead_dims = tensor.shape[:-1]
    flattened = tensor.reshape(-1, tensor.shape[-1])
    result = jnp.dot(flattened, weight, preferred_element_type=jnp.float32)
    return result.reshape(lead_dims + (weight.shape[1],))


def project_back(tensor, weight):
    lead_dims = tensor.shape[:-1]
    flattened = tensor.reshape(-1, tensor.shape[-1])
    result = lax.dot_general(
        flattened, weight, (((1,), (1,)), ((), ())), preferred_element_type=jnp.float32
    )
    return result.reshape(lead_dims + (weight.shape[0],))


def to_xlines(tensor):
    return lax.all_to_all(tensor, "gx", split_axis=1, concat_axis=0, tiled=True)


def from_xlines(tensor):
    return lax.all_to_all(tensor, "gx", split_axis=0, concat_axis=1, tiled=True)


def to_ylines(tensor):
    return lax.all_to_all(tensor, "gy", split_axis=0, concat_axis=1, tiled=True)


def from_ylines(tensor):
    return lax.all_to_all(tensor, "gy", split_axis=1, concat_axis=0, tiled=True)


def heads_of(tensor, which_part):
    lead_dims = tensor.shape[:-1]
    block_part = tensor[..., which_part * D : (which_part + 1) * D]
    return block_part.reshape(lead_dims + (HEADS, D // HEADS))


def softmax_rows(queries, key_part, layout, key_layout):
    scores = jnp.einsum(
        layout + "hd," + key_layout + "hd->bzhqk",
        queries,
        key_part,
        preferred_element_type=jnp.float32,
    )
    scores = scores * (D // HEADS) ** (-0.5)
    highest = jnp.max(scores, -1, keepdims=True)
    exponent = jnp.exp(scores - highest)
    return exponent / jnp.sum(exponent, -1, keepdims=True)


def attend(qkv_proj, layout):
    key_layout = layout.replace("q", "k")
    queries, key_part, value_part = (
        heads_of(qkv_proj, 0),
        heads_of(qkv_proj, 1),
        heads_of(qkv_proj, 2),
    )
    probs_low = softmax_rows(queries, key_part, layout, key_layout).astype(jnp.bfloat16)
    result = jnp.einsum(
        "bzhqk," + key_layout + "hd->" + layout + "hd",
        probs_low,
        value_part,
        preferred_element_type=jnp.float32,
    )
    return result.reshape(qkv_proj.shape[:-1] + (D,)).astype(jnp.bfloat16)


def attend_back(qkv_proj, grad_out, layout):
    key_layout = layout.replace("q", "k")
    scale = (D // HEADS) ** (-0.5)
    queries, key_part, value_part = (
        heads_of(qkv_proj, 0),
        heads_of(qkv_proj, 1),
        heads_of(qkv_proj, 2),
    )
    probs = softmax_rows(queries, key_part, layout, key_layout)
    probs_low = probs.astype(jnp.bfloat16)
    grad_heads = heads_of(grad_out, 0)
    grad_probs = jnp.einsum(
        layout + "hd," + key_layout + "hd->bzhqk",
        grad_heads,
        value_part,
        preferred_element_type=jnp.float32,
    )
    grad_scores = probs * (grad_probs - jnp.sum(probs * grad_probs, -1, keepdims=True))
    grad_low = grad_scores.astype(jnp.bfloat16)
    grad_q = jnp.einsum(
        "bzhqk," + key_layout + "hd->" + layout + "hd",
        grad_low,
        key_part,
        preferred_element_type=jnp.float32,
    )
    grad_k = jnp.einsum(
        "bzhqk," + layout + "hd->" + key_layout + "hd",
        grad_low,
        queries,
        preferred_element_type=jnp.float32,
    )
    grad_v = jnp.einsum(
        "bzhqk," + layout + "hd->" + key_layout + "hd",
        probs_low,
        grad_heads,
        preferred_element_type=jnp.float32,
    )
    lead_dims = qkv_proj.shape[:-1] + (D,)
    return jnp.concatenate(
        [
            (grad_q * scale).astype(jnp.bfloat16).reshape(lead_dims),
            (grad_k * scale).astype(jnp.bfloat16).reshape(lead_dims),
            grad_v.astype(jnp.bfloat16).reshape(lead_dims),
        ],
        -1,
    )


def mix_lines(stream, norm_gain, w_qkv, w_out, layout):
    stream_f = stream.astype(jnp.float32)
    normed = layer_norm(stream_f, norm_gain).astype(jnp.bfloat16)
    qkv_lines = project(normed, w_qkv).astype(jnp.bfloat16)
    mixed_out = attend(qkv_lines, layout)
    updated = to_low(stream_f + project(mixed_out, w_out))
    return (updated, qkv_lines)


def back_lines(stream, gradient, qkv_lines, norm_gain, w_qkv, w_out, layout):
    grad_mixed = project_back(gradient, w_out).astype(jnp.bfloat16)
    grad_qkv = attend_back(qkv_lines, grad_mixed, layout)
    grad_normed = project_back(grad_qkv, w_qkv)
    return to_low(
        gradient.astype(jnp.float32) + norm_back(stream.astype(jnp.float32), norm_gain, grad_normed)
    )


def mlp_back(stream, cotangent, gain_mlp, w_up, w_down):
    stream_f = stream.astype(jnp.float32)
    normed = layer_norm(stream_f, gain_mlp).astype(jnp.bfloat16)
    pre_act = project(normed, w_up)
    grad_act = project_back(cotangent, w_down).astype(jnp.bfloat16)
    _, pullback = jax.vjp(partial(jax.nn.gelu, approximate=True), pre_act)
    grad_pre = pullback(grad_act.astype(jnp.float32))[0].astype(jnp.bfloat16)
    return to_low(
        cotangent.astype(jnp.float32) + norm_back(stream_f, gain_mlp, project_back(grad_pre, w_up))
    )


def local(
    tokens, cotangent, gain_x, w_qkv_x, w_out_x, gain_y, w_qkv_y, w_out_y, gain_mlp, w_up, w_down
):
    tokens_x = to_xlines(tokens)
    cotangent_y = to_ylines(cotangent)
    stream_1x, qkv_x = mix_lines(tokens_x, gain_x, w_qkv_x, w_out_x, "qbz")
    stream_1 = to_ylines(from_xlines(stream_1x))
    stream_2, qkv_y = mix_lines(stream_1, gain_y, w_qkv_y, w_out_y, "bqz")
    grad_2 = mlp_back(stream_2, cotangent_y, gain_mlp, w_up, w_down)
    grad_1y = back_lines(stream_1, grad_2, qkv_y, gain_y, w_qkv_y, w_out_y, "bqz")
    grad_1 = to_xlines(from_ylines(grad_1y))
    grad_x = back_lines(tokens_x, grad_1, qkv_x, gain_x, w_qkv_x, w_out_x, "qbz")
    return from_xlines(grad_x)


def solution(mesh):
    in_specs = (
        P("gx", "gy", None, None),
        P("gx", "gy", None, None),
        P(),
        P(),
        P(),
        P(),
        P(),
        P(),
        P(),
        P(),
        P(),
    )
    out_specs = P("gx", "gy", None, None)
    return jax.shard_map(local, mesh=mesh, in_specs=in_specs, out_specs=out_specs, check_vma=False)
```

profile of v0, /device:TPU:24, one launch (start us, length us, event | category | flops | bytes accessed | tf_op | source)
XLA Modules:
  0.0 229.5 jit_solution(3078606832670182966)
XLA Ops:
  0.0 1.7 copy.222
  1.7 29.5 %all_to_all.93 = bf16[16,16,2,512]{3,2,0,1:T(2,128)(2,1)S(1)} all-to-all(bf16[16,16,2,512]{3,2,0,1:T(2,128)(2,1)S(1)} %copy.222), channel_id=1, replica_groups=mesh['gx'=16,'gy'=16] {'gx'}, dimensions={1} | all-to-all | bytes 1048576 | tf_op jit(solution)/shard_map/all_to_all | solution.py:44
  31.1 0.5 fusion.88
  32.1 1.0 multiply_reduce_fusion.7
  33.4 0.4 convert_bitcast_fusion
  34.0 2.4 %fusion.18 = bf16[256,1,2,1536]{3,0,2,1:T(8,128)(2,1)S(1)} fusion(bf16[512,1536]{1,0:T(8,128)(2,1)} %param.14, f32[256,2,512]{2,0,1:T(8,128)S(1)} %bitcast.211, f32[512]{0:T(512)S(1)} %copy-done.21, f32[256,2]{0,1:T(2,128)S(1)} %rsqrt.36, f32[256,2]{0,1:T(2,128)S(1)} %div.94), kind=kOutput, calls=%fused_computation.29 | convolution fusion | flops 807141376 | bytes 4200448 | tf_op jit(solution)/shard_map/dot_general | solution.py:30
  36.5 1.2 fusion.126
  37.7 2.1 copy.229
  39.8 2.1 copy.228
  41.8 2.0 copy.227
  43.9 4.6 %fusion.127 = (f32[2,8,256]{2,1,0:T(8,128)S(1)}, f32[2,8,256,256]{2,3,1,0:T(8,128)}) fusion(bf16[256,2,8,64]{0,3,2,1:T(8,128)(2,1)} %bitcast.225, bf16[256,2,8,64]{0,3,2,1:T(8,128)(2,1)} %bitcast.223), kind=kOutput, calls=%fused_computation.157 | convolution fusion | flops 137363712 | bytes 5259264 | tf_op jit(solution)/shard_map/sub | solution.py:74
  48.5 2.9 %convolution_convert_fusion.8 = bf16[2,8,64,256]{3,2,1,0:T(8,128)(2,1)S(1)} fusion(bf16[256,2,8,64]{0,3,2,1:T(8,128)(2,1)} %bitcast.237, f32[2,8,256,256]{2,3,1,0:T(8,128)} %get-tuple-element.12, f32[2,8,256]{2,1,0:T(8,128)S(1)} %get-tuple-element.11), kind=kOutput, calls=%fused_computation.79 | convolution fusion | flops 136577024 | bytes 5259264 | tf_op jit(solution)/shard_map/bzhqk,kbzhd->qbzhd/dot_general | solution.py:86
  51.4 0.5 fusion.76
  51.9 0.5 copy.232
  52.5 21.3 %all_to_all.94 = bf16[256,1,2,512]{3,2,1,0:T(2,128)(2,1)} all-to-all(bf16[256,1,2,512]{3,2,1,0:T(2,128)(2,1)S(1)} %copy.232), channel_id=1, replica_groups=mesh['gx'=16,'gy'=16] {'gx'}, dimensions={0} | all-to-all | bytes 1048576 | tf_op jit(solution)/shard_map/all_to_all | solution.py:48
  73.7 4.7 %all-to-all-start = ((bf16[16,16,2,512]{3,2,1,0:T(2,128)(2,1)}), bf16[16,16,2,512]{3,2,1,0:T(2,128)(2,1)}, u32[]{:S(2)}, u32[]{:S(2)}) async-start(bf16[16,16,2,512]{3,2,1,0:T(2,128)(2,1)} %param.12), calls=%async_computation | async-start | bytes 1048576 | tf_op jit(solution)/shard_map/all_to_all | solution.py:52
  78.4 2.1 copy.285
  80.6 6.6 %all-to-all-done = bf16[16,16,2,512]{3,2,1,0:T(2,128)(2,1)} async-done(((bf16[16,16,2,512]{3,2,1,0:T(2,128)(2,1)}), bf16[16,16,2,512]{3,2,1,0:T(2,128)(2,1)}, u32[]{:S(2)}, u32[]{:S(2)}) %all-to-all-start) | async-done | bytes 524320 | tf_op jit(solution)/shard_map/all_to_all | solution.py:52
  87.1 6.3 %all-to-all-start.3 = ((bf16[16,16,2,512]{3,1,2,0:T(8,128)(2,1)}), bf16[16,16,2,512]{3,1,2,0:T(8,128)(2,1)}, u32[]{:S(2)}, u32[]{:S(2)}) async-start(bf16[16,16,2,512]{3,1,2,0:T(8,128)(2,1)} %bitcast.218), calls=%async_computation.3 | async-start | bytes 1048576 | tf_op jit(solution)/shard_map/all_to_all | solution.py:52
  93.5 1.1 copy.221
  94.6 2.2 copy.220
  96.8 2.7 %convolution_convert_fusion.2 = bf16[256,2,2048]{2,0,1:T(8,128)(2,1)} fusion(bf16[256,2,512]{2,0,1:T(8,128)(2,1)S(1)} %bitcast.247, bf16[2048,512]{1,0:T(8,128)(2,1)S(1)} %copy-done), kind=kOutput, calls=%fused_computation.28 | convolution fusion | flops 1074790400 | bytes 4718592 | tf_op jit(solution)/shard_map/dot_general | solution.py:37
  99.5 2.7 %all-to-all-done.3 = bf16[16,16,2,512]{3,1,2,0:T(8,128)(2,1)} async-done(((bf16[16,16,2,512]{3,1,2,0:T(8,128)(2,1)}), bf16[16,16,2,512]{3,1,2,0:T(8,128)(2,1)}, u32[]{:S(2)}, u32[]{:S(2)}) %all-to-all-start.3) | async-done | bytes 524320 | tf_op jit(solution)/shard_map/all_to_all | solution.py:52
  102.2 1.2 convert_reduce_fusion.1
  103.5 1.3 multiply_reduce_fusion.6
  104.9 1.2 copy.234
  106.3 2.4 %fusion.19 = bf16[1,256,2,1536]{3,1,2,0:T(8,128)(2,1)S(1)} fusion(bf16[256,2,512]{2,0,1:T(8,128)(2,1)S(1)} %multiply_convert_fusion.2, bf16[512,1536]{1,0:T(8,128)(2,1)} %param.17), kind=kOutput, calls=%fused_computation.30 | convolution fusion | flops 806092800 | bytes 3670016 | tf_op jit(solution)/shard_map/dot_general | solution.py:30
  108.7 1.1 fusion.125
  110.0 1.4 copy.241
  111.5 2.3 copy.240
  113.7 3.5 %fusion.128 = (f32[2,8,256]{2,1,0:T(8,128)S(1)}, f32[2,8,256,256]{2,3,1,0:T(8,128)}) fusion(bf16[256,2,8,64]{0,3,2,1:T(8,128)(2,1)S(1)} %bitcast.229, bf16[256,2,8,64]{0,3,2,1:T(8,128)(2,1)S(1)} %bitcast.227), kind=kOutput, calls=%fused_computation.158 | convolution fusion | flops 137363712 | bytes 5259264 | tf_op jit(solution)/shard_map/sub | solution.py:74
  117.2 2.9 %convolution_convert_fusion.7 = bf16[2,8,64,256]{3,2,1,0:T(8,128)(2,1)S(1)} fusion(bf16[256,2,8,64]{0,3,2,1:T(8,128)(2,1)} %bitcast.239, f32[2,8,256,256]{2,3,1,0:T(8,128)} %get-tuple-element.14, f32[2,8,256]{2,1,0:T(8,128)S(1)} %get-tuple-element.13), kind=kOutput, calls=%fused_computation.78 | convolution fusion | flops 136577024 | bytes 5259264 | tf_op jit(solution)/shard_map/bzhqk,bkzhd->bqzhd/dot_general | solution.py:86
  120.1 0.5 fusion.75
  121.1 7.9 %fusion.80 = (f32[256,2]{0,1:T(2,128)S(1)}, f32[256,2,512]{2,0,1:T(8,128)}) fusion(bf16[1,256,2,512]{3,1,2,0:T(8,128)(2,1)S(1)} %fusion.75, f32[256,2]{0,1:T(2,128)S(1)} %broadcast_multiply_fusion.1, f32[512]{0:T(512)S(1)} %copy-done.20, bf16[512,2048]{1,0:T(8,128)(2,1)} %param.20, bf16[256,2,2048]{2,0,1:T(8,128)(2,1)} %convolution_convert_fusion.2, ...), kind=kOutput, calls=%fused_computation.91 | convolution fusion | flops 2172124672 | bytes 5775360 | tf_op jit(solution)/shard_map/dot_general | solution.py:37
  129.0 1.7 fusion.106
  130.7 1.9 fusion.82
  132.6 0.5 convolution_convert_fusion.4
  133.1 1.1 copy.245
  134.2 4.1 %convolution_convert_fusion.6 = bf16[2,8,64,256]{3,2,1,0:T(8,128)(2,1)} fusion(bf16[256,2,8,64]{0,3,2,1:T(8,128)(2,1)} %bitcast.243, f32[2,8,256,256]{2,3,1,0:T(8,128)} %get-tuple-element.14, f32[2,8,256]{2,1,0:T(8,128)S(1)} %get-tuple-element.13), kind=kOutput, calls=%fused_computation.77 | convolution fusion | flops 136577024 | bytes 5259264 | tf_op jit(solution)/shard_map/bzhqk,bqzhd->bkzhd/dot_general | solution.py:126
  138.3 1.1 multiply_reduce_fusion.1
  139.4 0.9 multiply_convert_fusion.1
  140.5 1.6 fusion.70
  142.1 1.3 fusion.69
  143.4 1.3 copy.251
  144.6 2.0 copy.249
  146.7 2.0 copy.250
  148.7 2.8 %multiply_reduce_fusion.5 = (f32[256,2]{0,1:T(2,128)S(1)}, f32[256,2,512]{2,0,1:T(8,128)S(1)}) fusion(f32[16,16,2,512]{3,1,0,2:T(8,128)S(1)} %copy.234, f32[256,2]{0,1:T(2,128)S(1)} %div.99, f32[512]{0:T(512)S(1)} %copy-done.19, bf16[512,1536]{1,0:T(8,128)(2,1)} %param.17, bf16[256,2,512]{2,0,1:T(8,128)(2,1)S(1)} %copy.251, ...), kind=kOutput, calls=%fused_computation.100 | convolution fusion | flops 811073024 | bytes 5249024 | tf_op jit(solution)/shard_map/dot_general | solution.py:37
  152.4 0.5 copy.252
  152.9 13.5 %all_to_all.95 = bf16[1,256,2,512]{3,2,0,1:T(2,128)(2,1)S(1)} all-to-all(bf16[1,256,2,512]{3,2,0,1:T(2,128)(2,1)S(1)} %copy.252), channel_id=1, replica_groups=mesh['gx'=16,'gy'=16] {'gy'}, dimensions={1} | all-to-all | bytes 1048576 | tf_op jit(solution)/shard_map/all_to_all | solution.py:56
  166.7 22.4 %all_to_all.96 = bf16[16,16,2,512]{3,0,2,1:T(8,128)(2,1)S(1)} all-to-all(bf16[16,16,2,512]{3,0,2,1:T(8,128)(2,1)S(1)} %copy.253), channel_id=1, replica_groups=mesh['gx'=16,'gy'=16] {'gx'}, dimensions={1} | all-to-all | bytes 1048576 | tf_op jit(solution)/shard_map/all_to_all | solution.py:44
  189.1 0.8 copy-done.2
  189.9 0.5 convolution_convert_fusion.3
  190.6 3.9 %convolution_convert_fusion.5 = bf16[2,8,64,256]{3,2,1,0:T(8,128)(2,1)} fusion(bf16[256,2,8,64]{0,3,2,1:T(8,128)(2,1)S(1)} %bitcast.245, f32[2,8,256,256]{2,3,1,0:T(8,128)} %get-tuple-element.12, f32[2,8,256]{2,1,0:T(8,128)S(1)} %get-tuple-element.11), kind=kOutput, calls=%fused_computation.76 | convolution fusion | flops 136577024 | bytes 5259264 | tf_op jit(solution)/shard_map/bzhqk,qbzhd->kbzhd/dot_general | solution.py:126
  194.5 0.8 multiply_reduce_fusion
  195.4 0.9 multiply_convert_fusion
  196.4 1.6 fusion.72
  198.0 1.3 fusion.71
  199.3 1.3 copy.261
  200.5 1.3 copy.259
  201.8 1.3 copy.260
  203.0 2.6 %multiply_reduce_fusion.4 = (f32[256,2]{0,1:T(2,128)S(1)}, f32[256,2,512]{2,0,1:T(8,128)S(1)}) fusion(f32[256,2,512]{2,0,1:T(8,128)S(1)} %bitcast.213, f32[256,2]{0,1:T(2,128)S(1)} %div.94, f32[512]{0:T(512)S(1)} %copy-done.21, bf16[512,1536]{1,0:T(8,128)(2,1)} %param.14, bf16[256,2,512]{2,0,1:T(8,128)(2,1)S(1)} %copy.261, ...), kind=kOutput, calls=%fused_computation.99 | convolution fusion | flops 811073024 | bytes 5249024 | tf_op jit(solution)/shard_map/dot_general | solution.py:37
  206.4 0.5 copy.262
  207.0 21.2 %all_to_all.97 = bf16[256,1,2,512]{3,2,1,0:T(2,128)(2,1)S(1)} all-to-all(bf16[256,1,2,512]{3,2,1,0:T(2,128)(2,1)S(1)} %copy.262), channel_id=1, replica_groups=mesh['gx'=16,'gy'=16] {'gx'}, dimensions={0} | all-to-all | bytes 1048576 | tf_op jit(solution)/shard_map/all_to_all | solution.py:48
  228.2 1.3 copy.284
  (77 shorter events, 4.5 us)
Async XLA Ops:
  0.0 96.8 %copy-start = (bf16[2048,512]{1,0:T(8,128)(2,1)S(1)}, bf16[2048,512]{1,0:T(8,128)(2,1)}, u32[]{:S(2)}) copy-start(bf16[2048,512]{1,0:T(8,128)(2,1)} %param.21) | copy-start | bytes 6291460
  0.0 34.0 %copy-start.21 = (f32[512]{0:T(512)S(1)}, f32[512]{0:T(512)}, u32[]{:S(2)}) copy-start(f32[512]{0:T(512)} %param.13) | copy-start | bytes 6148
  48.5 2.9 %copy-start.8 = (bf16[512,512]{1,0:T(8,128)(2,1)S(1)}, bf16[512,512]{1,0:T(8,128)(2,1)}, u32[]{:S(2)}) copy-start(bf16[512,512]{1,0:T(8,128)(2,1)} %param.15) | copy-start | bytes 1572868
  73.7 13.4 %all-to-all-start = ((bf16[16,16,2,512]{3,2,1,0:T(2,128)(2,1)}), bf16[16,16,2,512]{3,2,1,0:T(2,128)(2,1)}, u32[]{:S(2)}, u32[]{:S(2)}) async-start(bf16[16,16,2,512]{3,2,1,0:T(2,128)(2,1)} %param.12), calls=%async_computation | async-start | bytes 1048576 | tf_op jit(solution)/shard_map/all_to_all | solution.py:52
  87.1 15.1 %all-to-all-start.3 = ((bf16[16,16,2,512]{3,1,2,0:T(8,128)(2,1)}), bf16[16,16,2,512]{3,1,2,0:T(8,128)(2,1)}, u32[]{:S(2)}, u32[]{:S(2)}) async-start(bf16[16,16,2,512]{3,1,2,0:T(8,128)(2,1)} %bitcast.218), calls=%async_computation.3 | async-start | bytes 1048576 | tf_op jit(solution)/shard_map/all_to_all | solution.py:52
  96.8 9.3 %copy-start.19 = (f32[512]{0:T(512)S(1)}, f32[512]{0:T(512)}, u32[]{:S(2)}) copy-start(f32[512]{0:T(512)} %param.16) | copy-start | bytes 6148
  110.0 7.2 %copy-start.12 = (bf16[1,256,2,512]{1,3,2,0:T(8,128)(2,1)}, bf16[1,256,2,512]{1,3,2,0:T(8,128)(2,1)S(1)}, u32[]{:S(2)}) copy-start(bf16[1,256,2,512]{1,3,2,0:T(8,128)(2,1)S(1)} %copy.242) | copy-start | bytes 1572868
  111.5 8.7 %copy-start.14 = (bf16[1,256,2,512]{1,3,2,0:T(8,128)(2,1)}, bf16[1,256,2,512]{1,3,2,0:T(8,128)(2,1)S(1)}, u32[]{:S(2)}) copy-start(bf16[1,256,2,512]{1,3,2,0:T(8,128)(2,1)S(1)} %copy.241) | copy-start | bytes 1572868
  117.2 2.9 %copy-start.6 = (bf16[512,512]{1,0:T(8,128)(2,1)S(1)}, bf16[512,512]{1,0:T(8,128)(2,1)}, u32[]{:S(2)}) copy-start(bf16[512,512]{1,0:T(8,128)(2,1)} %param.18) | copy-start | bytes 1572868
  117.2 3.9 %copy-start.20 = (f32[512]{0:T(512)S(1)}, f32[512]{0:T(512)}, u32[]{:S(2)}) copy-start(f32[512]{0:T(512)} %param.19) | copy-start | bytes 6148
  129.0 3.7 %copy-start.7 = (bf16[512,512]{1,0:T(8,128)(2,1)S(1)}, bf16[512,512]{1,0:T(8,128)(2,1)}, u32[]{:S(2)}) copy-start(bf16[512,512]{1,0:T(8,128)(2,1)} %param.18) | copy-start | bytes 1572868
  134.2 4.1 %copy-start.5 = (f32[2,8,256,256]{2,3,1,0:T(8,128)S(1)}, f32[2,8,256,256]{2,3,1,0:T(8,128)}, u32[]{:S(2)}) copy-start(f32[2,8,256,256]{2,3,1,0:T(8,128)} %get-tuple-element.14) | copy-start | bytes 12582916
  134.2 4.1 %copy-start.17 = (bf16[1,256,2,512]{1,3,2,0:T(8,128)(2,1)S(1)}, bf16[1,256,2,512]{1,3,2,0:T(8,128)(2,1)}, u32[]{:S(2)}) copy-start(bf16[1,256,2,512]{1,3,2,0:T(8,128)(2,1)} %copy.240) | copy-start | bytes 1572868
  134.2 4.1 %copy-start.18 = (bf16[256,2,512]{0,2,1:T(8,128)(2,1)S(1)}, bf16[256,2,512]{0,2,1:T(8,128)(2,1)}, u32[]{:S(2)}) copy-start(bf16[256,2,512]{0,2,1:T(8,128)(2,1)} %copy.245) | copy-start | bytes 1572868
  139.4 1.0 copy-start.15
  139.4 2.7 %copy-start.13 = (bf16[1,256,2,512]{1,3,2,0:T(8,128)(2,1)S(1)}, bf16[1,256,2,512]{1,3,2,0:T(8,128)(2,1)}, u32[]{:S(2)}) copy-start(bf16[1,256,2,512]{1,3,2,0:T(8,128)(2,1)} %copy-done.12) | copy-start | bytes 1572868
  152.0 37.9 %copy-start.9 = (bf16[512,512]{1,0:T(8,128)(2,1)S(1)}, bf16[512,512]{1,0:T(8,128)(2,1)}, u32[]{:S(2)}) copy-start(bf16[512,512]{1,0:T(8,128)(2,1)} %param.15) | copy-start | bytes 1572868
  189.1 0.8 copy-start.2
  190.6 3.9 %copy-start.4 = (f32[2,8,256,256]{2,3,1,0:T(8,128)S(1)}, f32[2,8,256,256]{2,3,1,0:T(8,128)}, u32[]{:S(2)}) copy-start(f32[2,8,256,256]{2,3,1,0:T(8,128)} %get-tuple-element.12) | copy-start | bytes 12582916
  190.6 3.9 %copy-start.16 = (bf16[256,1,2,512]{0,3,2,1:T(8,128)(2,1)S(1)}, bf16[256,1,2,512]{0,3,2,1:T(8,128)(2,1)}, u32[]{:S(2)}) copy-start(bf16[256,1,2,512]{0,3,2,1:T(8,128)(2,1)} %copy.227) | copy-start | bytes 1572868
  195.4 1.0 copy-start.11
  195.4 2.6 %copy-start.10 = (bf16[256,1,2,512]{0,3,2,1:T(8,128)(2,1)S(1)}, bf16[256,1,2,512]{0,3,2,1:T(8,128)(2,1)}, u32[]{:S(2)}) copy-start(bf16[256,1,2,512]{0,3,2,1:T(8,128)(2,1)} %copy.229) | copy-start | bytes 1572868
  203.0 3.0 %copy-start.3 = (bf16[16,16,1,2,512]{4,1,0,3,2:T(8,128)(2,1)S(1)}, bf16[16,16,1,2,512]{4,1,0,3,2:T(8,128)(2,1)}, u32[]{:S(2)}) copy-start(bf16[16,16,1,2,512]{4,1,0,3,2:T(8,128)(2,1)} %copy-done.2) | copy-start | bytes 1572868
  205.6 23.9 %copy-start.1 = (bf16[2048,512]{1,0:T(8,128)(2,1)S(1)}, bf16[2048,512]{1,0:T(8,128)(2,1)}, u32[]{:S(2)}) copy-start(bf16[2048,512]{1,0:T(8,128)(2,1)} %param.21) | copy-start | bytes 6291460
where the time goes:
time: 231 us; the launch traced here: 229 us
  blocking collectives  108 us (47%)
  matrix products  52.3 us (23%)
  local copies, waits for them, and re-layouts  36.4 us (16%)
  other arithmetic  12.2 us (5%)
  starting transfers between devices  11 us (5%)
  waiting for transfers between devices  9.24 us (4%)
    all_to_all x2, blocking collectives, to_xlines(): return lax.all_to_all(tensor, 'gx', split_axis=1, concat_axis=0, tiled=True)  51.8 us
    all_to_all x2, blocking collectives, from_xlines(): return lax.all_to_all(tensor, 'gx', split_axis=0, concat_axis=1, tiled=True)  42.5 us
    dot_general x6, matrix products, project_back(): lax.dot_general(flattened, weight, (((1,), (1,)), ((), ())), preferred_el...  17 us
    all_to_all x1, blocking collectives, from_ylines(): return lax.all_to_all(tensor, 'gy', split_axis=1, concat_axis=0, tiled=True)  13.5 us
    slice x8, local copies, waits for them, and re-layouts, heads_of(): block_part = tensor[..., which_part * D:(which_part + 1) * D]  12.4 us
    all_to_all x2, starting transfers between devices, to_ylines(): return lax.all_to_all(tensor, 'gy', split_axis=0, concat_axis=1, tiled=True)  11 us
    all_to_all x2, waiting for transfers between devices, to_ylines(): return lax.all_to_all(tensor, 'gy', split_axis=0, concat_axis=1, tiled=True)  9.24 us
    concatenate x6, local copies, waits for them, and re-layouts, attend_back(): jnp.concatenate([(grad_q * scale).astype(jnp.bfloat16).reshape(lead_dims)...  9.1 us
  transfers between devices with their start and end apart: 2, of which 2 were waited for; matrix products, arithmetic and copies ran while one was open for 4% of the time, Pallas kernels for 0%

commit v1 on v0

--- a/solution.py
+++ b/solution.py
@@ -1,3 +1,4 @@
+import functools
 from functools import partial
 import jax
 import jax.numpy as jnp
@@ -8,6 +9,21 @@
 HEADS = 8
 
 
+def extend_racks_here(load, a_name):
+    return jnp.concatenate(
+        lax.all_to_all(
+            jnp.stack(jnp.split(load, lax.axis_size(a_name), 0), axis=0),
+            axis_name=a_name,
+            split_axis=0,
+            concat_axis=0,
+        ),
+        1,
+    )
+
+
+cubes_store = functools.partial(extend_racks_here, a_name="gx")
+
+
 def to_low(tensor):
     return lax.optimization_barrier(tensor.astype(jnp.bfloat16))
 
@@ -45,7 +61,7 @@
 
 
 def from_xlines(tensor):
-    return lax.all_to_all(tensor, "gx", split_axis=0, concat_axis=1, tiled=True)
+    return cubes_store(tensor)
 
 
 def to_ylines(tensor):

time: 231 us -> 214 us (0.926)
  local copies, waits for them, and re-layouts: 36.4 us -> 23 us
  other arithmetic: 12.2 us -> 8.71 us
  waiting for transfers between devices: 9.24 us -> 11.9 us
    slice x8, local copies, waits for them, and re-layouts: 12.4 us -> 8.03 us  [heads_of(): block_part = tensor[..., which_part * D:(which_part + 1) * D]]
    all_to_all x2 -> x0, local copies, waits for them, and re-layouts: 3.42 us -> none  [from_xlines(): return lax.all_to_all(tensor, 'gx', split_axis=0, concat_axis=1, tiled=True)]
    concatenate x6, local copies, waits for them, and re-layouts: 9.1 us -> 5.99 us  [attend_back(): jnp.concatenate([(grad_q * scale).astype(jnp.bfloat16).reshape(lead_dims)...]
    reshape x0 -> x2, local copies, waits for them, and re-layouts: none -> 2.7 us  [extend_racks_here(): jnp.concatenate(lax.all_to_all(jnp.stack(jnp.split(load, lax.axis_size(a_...]
    all_to_all x2, waiting for transfers between devices: 9.24 us -> 11.9 us  [to_ylines(): return lax.all_to_all(tensor, 'gy', split_axis=0, concat_axis=1, tiled=True)]
  transfers between devices with their start and end apart: 2 -> 2, of which waited for: 2 -> 2; matrix products, arithmetic and copies ran while one was open for 4% -> 2% of each run, Pallas kernels for 0% -> 0%
where the time goes in v1:
time: 214 us; the launch traced here: 213 us
  blocking collectives  108 us (50%)
  matrix products  50 us (23%)
  local copies, waits for them, and re-layouts  23 us (11%)
  waiting for transfers between devices  11.9 us (6%)
  starting transfers between devices  10.4 us (5%)
  other arithmetic  8.71 us (4%)
    all_to_all x2, blocking collectives, to_xlines(): return lax.all_to_all(tensor, 'gx', split_axis=1, concat_axis=0, tiled=True)  51.9 us
    all_to_all x2, blocking collectives, extend_racks_here(): lax.all_to_all(jnp.stack(jnp.split(load, lax.axis_size(a_name), 0), axis=...  42.4 us
    dot_general x6, matrix products, project_back(): lax.dot_general(flattened, weight, (((1,), (1,)), ((), ())), preferred_el...  17.1 us
    all_to_all x1, blocking collectives, from_ylines(): return lax.all_to_all(tensor, 'gy', split_axis=1, concat_axis=0, tiled=True)  13.5 us
    all_to_all x2, waiting for transfers between devices, to_ylines(): return lax.all_to_all(tensor, 'gy', split_axis=0, concat_axis=1, tiled=True)  11.9 us
    all_to_all x2, starting transfers between devices, to_ylines(): return lax.all_to_all(tensor, 'gy', split_axis=0, concat_axis=1, tiled=True)  10.4 us
    sub x2, matrix products, softmax_rows(): exponent = jnp.exp(scores - highest)  8.14 us
    slice x8, local copies, waits for them, and re-layouts, heads_of(): block_part = tensor[..., which_part * D:(which_part + 1) * D]  8.03 us
  transfers between devices with their start and end apart: 2, of which 2 were waited for; matrix products, arithmetic and copies ran while one was open for 2% of the time, Pallas kernels for 0%

profile of v1, /device:TPU:24, one launch (start us, length us, event | category | flops | bytes accessed | tf_op | source)
XLA Modules:
  0.0 212.6 jit_solution(18235330908141287686)
XLA Ops:
  0.0 1.7 copy.173
  1.7 29.5 %all_to_all.67 = bf16[16,16,2,512]{3,2,0,1:T(2,128)(2,1)S(1)} all-to-all(bf16[16,16,2,512]{3,2,0,1:T(2,128)(2,1)S(1)} %copy.173), channel_id=1, replica_groups=mesh['gx'=16,'gy'=16] {'gx'}, dimensions={1} | all-to-all | bytes 1048576 | tf_op jit(solution)/shard_map/all_to_all | solution.py:60
  31.4 0.3 multiply_reduce_fusion.7
  32.1 2.8 %fusion.18 = bf16[256,1,2,1536]{3,0,2,1:T(8,128)(2,1)S(1)} fusion(bf16[512,1536]{1,0:T(8,128)(2,1)} %param.14, f32[256,2,512]{2,0,1:T(8,128)S(1)} %bitcast.332, f32[512]{0:T(512)S(1)} %copy-done.23, f32[256,2]{0,1:T(2,128)S(1)} %rsqrt.36, f32[256,2]{0,1:T(2,128)S(1)} %div.94), kind=kOutput, calls=%fused_computation.29 | convolution fusion | flops 807141376 | bytes 4200448 | tf_op jit(solution)/shard_map/dot_general | solution.py:46
  34.9 1.2 fusion.126
  36.1 2.0 copy.183
  38.2 2.0 copy.182
  40.2 2.0 copy.181
  42.2 4.6 %fusion.127 = (f32[2,8,256]{2,1,0:T(8,128)S(1)}, f32[2,8,256,256]{2,3,1,0:T(8,128)}) fusion(bf16[256,2,8,64]{0,3,2,1:T(8,128)(2,1)} %bitcast.346, bf16[256,2,8,64]{0,3,2,1:T(8,128)(2,1)} %bitcast.344), kind=kOutput, calls=%fused_computation.220 | convolution fusion | flops 137363712 | bytes 5259264 | tf_op jit(solution)/shard_map/sub | solution.py:90
  46.9 2.9 %convolution_convert_fusion.8 = bf16[2,8,64,256]{3,2,1,0:T(8,128)(2,1)S(1)} fusion(bf16[256,2,8,64]{0,3,2,1:T(8,128)(2,1)} %bitcast.358, f32[2,8,256,256]{2,3,1,0:T(8,128)} %get-tuple-element.12, f32[2,8,256]{2,1,0:T(8,128)S(1)} %get-tuple-element.11), kind=kOutput, calls=%fused_computation.79 | convolution fusion | flops 136577024 | bytes 5259264 | tf_op jit(solution)/shard_map/bzhqk,kbzhd->qbzhd/dot_general | solution.py:102
  49.8 0.5 fusion.76
  50.5 21.2 %all_to_all.68 = bf16[16,16,1,2,512]{4,1,3,2,0:T(8,128)(2,1)S(1)} all-to-all(bf16[16,16,1,2,512]{4,1,3,2,0:T(8,128)(2,1)S(1)} %constant_dynamic-update-slice_fusion), channel_id=1, replica_groups=mesh['gx'=16,'gy'=16] {'gx'}, dimensions={0} | all-to-all | bytes 1048576 | tf_op jit(solution)/shard_map/all_to_all | solution.py:14
  71.6 4.7 %all-to-all-start = ((bf16[16,16,2,512]{3,2,1,0:T(2,128)(2,1)}), bf16[16,16,2,512]{3,2,1,0:T(2,128)(2,1)S(1)}, u32[]{:S(2)}, u32[]{:S(2)}) async-start(bf16[16,16,2,512]{3,2,1,0:T(2,128)(2,1)} %param.12), calls=%async_computation | async-start | bytes 1048576 | tf_op jit(solution)/shard_map/all_to_all | solution.py:68
  76.4 1.4 copy.186
  77.7 7.2 %all-to-all-done = bf16[16,16,2,512]{3,2,1,0:T(2,128)(2,1)S(1)} async-done(((bf16[16,16,2,512]{3,2,1,0:T(2,128)(2,1)}), bf16[16,16,2,512]{3,2,1,0:T(2,128)(2,1)S(1)}, u32[]{:S(2)}, u32[]{:S(2)}) %all-to-all-start) | async-done | bytes 524320 | tf_op jit(solution)/shard_map/all_to_all | solution.py:68
  84.9 5.7 %all-to-all-start.3 = ((bf16[16,16,2,512]{3,2,1,0:T(2,128)(2,1)}), bf16[16,16,2,512]{3,2,1,0:T(2,128)(2,1)S(1)}, u32[]{:S(2)}, u32[]{:S(2)}) async-start(bf16[16,16,2,512]{3,2,1,0:T(2,128)(2,1)} %copy.186), calls=%async_computation.3 | async-start | bytes 1048576 | tf_op jit(solution)/shard_map/all_to_all | solution.py:68
  90.8 1.1 copy.171
  91.9 2.7 %convolution_convert_fusion.2 = bf16[256,2,2048]{2,0,1:T(8,128)(2,1)} fusion(bf16[256,2,512]{2,0,1:T(8,128)(2,1)S(1)} %bitcast.368, bf16[2048,512]{1,0:T(8,128)(2,1)S(1)} %copy-done), kind=kOutput, calls=%fused_computation.28 | convolution fusion | flops 1074790400 | bytes 4718592 | tf_op jit(solution)/shard_map/dot_general | solution.py:53
  94.6 4.7 %all-to-all-done.3 = bf16[16,16,2,512]{3,2,1,0:T(2,128)(2,1)S(1)} async-done(((bf16[16,16,2,512]{3,2,1,0:T(2,128)(2,1)}), bf16[16,16,2,512]{3,2,1,0:T(2,128)(2,1)S(1)}, u32[]{:S(2)}, u32[]{:S(2)}) %all-to-all-start.3) | async-done | bytes 524320 | tf_op jit(solution)/shard_map/all_to_all | solution.py:68
  99.5 0.3 multiply_reduce_fusion.6
  99.9 0.2 multiply_convert_fusion.2
  100.2 2.4 %fusion.19 = bf16[1,256,2,1536]{3,1,2,0:T(8,128)(2,1)S(1)} fusion(bf16[256,2,512]{2,0,1:T(8,128)(2,1)S(1)} %multiply_convert_fusion.2, bf16[512,1536]{1,0:T(8,128)(2,1)} %param.17), kind=kOutput, calls=%fused_computation.30 | convolution fusion | flops 806092800 | bytes 3670016 | tf_op jit(solution)/shard_map/dot_general | solution.py:46
  102.7 0.2 copy.194
  102.9 0.2 copy.193
  103.1 0.2 copy.192
  103.4 3.5 %fusion.128 = (f32[2,8,256]{2,1,0:T(8,128)S(1)}, f32[2,8,256,256]{2,3,1,0:T(8,128)}) fusion(bf16[256,2,8,64]{0,3,2,1:T(8,128)(2,1)S(1)} %bitcast.350, bf16[256,2,8,64]{0,3,2,1:T(8,128)(2,1)S(1)} %bitcast.348), kind=kOutput, calls=%fused_computation.221 | convolution fusion | flops 137363712 | bytes 5259264 | tf_op jit(solution)/shard_map/sub | solution.py:90
  106.9 2.7 %convolution_convert_fusion.7 = bf16[2,8,64,256]{3,2,1,0:T(8,128)(2,1)S(1)} fusion(bf16[256,2,8,64]{0,3,2,1:T(8,128)(2,1)S(1)} %bitcast.360, f32[2,8,256,256]{2,3,1,0:T(8,128)} %get-tuple-element.14, f32[2,8,256]{2,1,0:T(8,128)S(1)} %get-tuple-element.13), kind=kOutput, calls=%fused_computation.78 | convolution fusion | flops 136577024 | bytes 5259264 | tf_op jit(solution)/shard_map/bzhqk,bkzhd->bqzhd/dot_general | solution.py:102
  109.8 0.5 fusion.75
  110.4 0.3 fusion.77
  110.7 8.0 %fusion.80 = (f32[256,2]{0,1:T(2,128)S(1)}, f32[256,2,512]{2,0,1:T(8,128)}) fusion(bf16[1,256,2,512]{3,1,2,0:T(8,128)(2,1)S(1)} %fusion.75, f32[256,2]{0,1:T(2,128)S(1)} %broadcast_multiply_fusion.1, f32[512]{0:T(512)S(1)} %copy-done.22, bf16[512,2048]{1,0:T(8,128)(2,1)} %param.20, bf16[256,2,2048]{2,0,1:T(8,128)(2,1)} %convolution_convert_fusion.2, ...), kind=kOutput, calls=%fused_computation.91 | convolution fusion | flops 2172124672 | bytes 5775360 | tf_op jit(solution)/shard_map/dot_general | solution.py:53
  118.8 1.7 fusion.106
  120.5 1.7 fusion.82
  122.2 0.5 convolution_convert_fusion.4
  122.9 3.1 %convolution_convert_fusion.6 = bf16[2,8,64,256]{3,2,1,0:T(8,128)(2,1)S(1)} fusion(bf16[256,2,8,64]{0,3,2,1:T(8,128)(2,1)S(1)} %bitcast.364, f32[2,8,256,256]{2,3,1,0:T(8,128)} %get-tuple-element.14, f32[2,8,256]{2,1,0:T(8,128)S(1)} %get-tuple-element.13), kind=kOutput, calls=%fused_computation.77 | convolution fusion | flops 136577024 | bytes 5259264 | tf_op jit(solution)/shard_map/bzhqk,bqzhd->bkzhd/dot_general | solution.py:142
  126.0 0.3 copy-done.8
  126.4 1.1 multiply_reduce_fusion.1
  127.5 0.9 multiply_convert_fusion.1
  128.5 0.8 fusion.70
  129.3 0.5 fusion.69
  129.8 1.0 copy.203
  130.8 0.2 copy.201
  131.0 1.0 copy.202
  132.0 2.8 %multiply_reduce_fusion.5 = (f32[256,2]{0,1:T(2,128)S(1)}, f32[256,2,512]{2,0,1:T(8,128)S(1)}) fusion(f32[256,2]{0,1:T(2,128)S(1)} %div.99, bf16[16,16,2,512]{3,2,1,0:T(2,128)(2,1)S(1)} %all-to-all-done.3, f32[512]{0:T(512)S(1)} %copy-done.21, bf16[512,1536]{1,0:T(8,128)(2,1)} %param.17, bf16[256,2,512]{2,0,1:T(8,128)(2,1)} %copy.203, ...), kind=kOutput, calls=%fused_computation.100 | convolution fusion | flops 811335168 | bytes 4724736 | tf_op jit(solution)/shard_map/dot_general | solution.py:53
  134.9 0.4 fusion.107
  135.3 0.4 fusion.81
  135.7 0.5 copy.204
  136.3 13.5 %all_to_all.69 = bf16[1,256,2,512]{3,2,0,1:T(2,128)(2,1)S(1)} all-to-all(bf16[1,256,2,512]{3,2,0,1:T(2,128)(2,1)S(1)} %copy.204), channel_id=1, replica_groups=mesh['gx'=16,'gy'=16] {'gy'}, dimensions={1} | all-to-all | bytes 1048576 | tf_op jit(solution)/shard_map/all_to_all | solution.py:72
  149.7 0.3 copy.205
  150.0 22.5 %all_to_all.70 = bf16[16,16,2,512]{3,0,2,1:T(8,128)(2,1)S(1)} all-to-all(bf16[16,16,2,512]{3,0,2,1:T(8,128)(2,1)S(1)} %copy.205), channel_id=1, replica_groups=mesh['gx'=16,'gy'=16] {'gx'}, dimensions={1} | all-to-all | bytes 1048576 | tf_op jit(solution)/shard_map/all_to_all | solution.py:60
  172.6 0.8 copy-done.4
  173.3 0.5 convolution_convert_fusion.3
  174.1 3.9 %convolution_convert_fusion.5 = bf16[2,8,64,256]{3,2,1,0:T(8,128)(2,1)} fusion(bf16[256,2,8,64]{0,3,2,1:T(8,128)(2,1)S(1)} %bitcast.366, f32[2,8,256,256]{2,3,1,0:T(8,128)} %get-tuple-element.12, f32[2,8,256]{2,1,0:T(8,128)S(1)} %get-tuple-element.11), kind=kOutput, calls=%fused_computation.76 | convolution fusion | flops 136577024 | bytes 5259264 | tf_op jit(solution)/shard_map/bzhqk,qbzhd->kbzhd/dot_general | solution.py:142
  178.0 0.8 multiply_reduce_fusion
  178.8 0.9 multiply_convert_fusion
  179.9 1.6 fusion.72
  181.4 1.3 fusion.71
  182.7 1.3 copy.213
  183.9 1.3 copy.211
  185.2 1.3 copy.212
  186.5 2.6 %multiply_reduce_fusion.4 = (f32[256,2]{0,1:T(2,128)S(1)}, f32[256,2,512]{2,0,1:T(8,128)S(1)}) fusion(f32[256,2,512]{2,0,1:T(8,128)S(1)} %bitcast.334, f32[256,2]{0,1:T(2,128)S(1)} %div.94, f32[512]{0:T(512)S(1)} %copy-done.23, bf16[512,1536]{1,0:T(8,128)(2,1)} %param.14, bf16[256,2,512]{2,0,1:T(8,128)(2,1)S(1)} %copy.213, ...), kind=kOutput, calls=%fused_computation.99 | convolution fusion | flops 811073024 | bytes 5249024 | tf_op jit(solution)/shard_map/dot_general | solution.py:53
  189.1 0.4 fusion.112
  189.5 0.4 fusion.87
  190.1 21.2 %all_to_all.71 = bf16[16,16,1,2,512]{4,1,3,2,0:T(8,128)(2,1)S(1)} all-to-all(bf16[16,16,1,2,512]{4,1,3,2,0:T(8,128)(2,1)S(1)} %constant_dynamic-update-slice_fusion.16), channel_id=1, replica_groups=mesh['gx'=16,'gy'=16] {'gx'}, dimensions={0} | all-to-all | bytes 1048576 | tf_op jit(solution)/shard_map/all_to_all | solution.py:14
  211.3 1.3 copy.214
  (108 shorter events, 2.5 us)
Async XLA Ops:
  0.0 91.9 %copy-start = (bf16[2048,512]{1,0:T(8,128)(2,1)S(1)}, bf16[2048,512]{1,0:T(8,128)(2,1)}, u32[]{:S(2)}) copy-start(bf16[2048,512]{1,0:T(8,128)(2,1)} %param.21) | copy-start | bytes 6291460
  0.0 32.1 %copy-start.23 = (f32[512]{0:T(512)S(1)}, f32[512]{0:T(512)}, u32[]{:S(2)}) copy-start(f32[512]{0:T(512)} %param.13) | copy-start | bytes 6148
  32.1 17.7 %copy-start.2 = (f32[16,16,1,2,512]{4,1,0,3,2:T(8,128)}, f32[16,16,1,2,512]{4,1,0,3,2:T(8,128)S(1)}, u32[]{:S(2)}) copy-start(f32[16,16,1,2,512]{4,1,0,3,2:T(8,128)S(1)} %copy.175) | copy-start | bytes 3145732
  46.9 2.9 %copy-start.10 = (bf16[512,512]{1,0:T(8,128)(2,1)S(1)}, bf16[512,512]{1,0:T(8,128)(2,1)}, u32[]{:S(2)}) copy-start(bf16[512,512]{1,0:T(8,128)(2,1)} %param.15) | copy-start | bytes 1572868
  71.6 13.3 %all-to-all-start = ((bf16[16,16,2,512]{3,2,1,0:T(2,128)(2,1)}), bf16[16,16,2,512]{3,2,1,0:T(2,128)(2,1)S(1)}, u32[]{:S(2)}, u32[]{:S(2)}) async-start(bf16[16,16,2,512]{3,2,1,0:T(2,128)(2,1)} %param.12), calls=%async_computation | async-start | bytes 1048576 | tf_op jit(solution)/shard_map/all_to_all | solution.py:68
  84.9 14.3 %all-to-all-start.3 = ((bf16[16,16,2,512]{3,2,1,0:T(2,128)(2,1)}), bf16[16,16,2,512]{3,2,1,0:T(2,128)(2,1)S(1)}, u32[]{:S(2)}, u32[]{:S(2)}) async-start(bf16[16,16,2,512]{3,2,1,0:T(2,128)(2,1)} %copy.186), calls=%async_computation.3 | async-start | bytes 1048576 | tf_op jit(solution)/shard_map/all_to_all | solution.py:68
  90.8 9.2 %copy-start.21 = (f32[512]{0:T(512)S(1)}, f32[512]{0:T(512)}, u32[]{:S(2)}) copy-start(f32[512]{0:T(512)} %param.16) | copy-start | bytes 6148
  102.9 6.7 %copy-start.14 = (bf16[1,256,2,512]{1,3,2,0:T(8,128)(2,1)}, bf16[1,256,2,512]{1,3,2,0:T(8,128)(2,1)S(1)}, u32[]{:S(2)}) copy-start(bf16[1,256,2,512]{1,3,2,0:T(8,128)(2,1)S(1)} %copy.194) | copy-start | bytes 1572868
  103.1 6.5 %copy-start.16 = (bf16[1,256,2,512]{1,3,2,0:T(8,128)(2,1)}, bf16[1,256,2,512]{1,3,2,0:T(8,128)(2,1)S(1)}, u32[]{:S(2)}) copy-start(bf16[1,256,2,512]{1,3,2,0:T(8,128)(2,1)S(1)} %copy.193) | copy-start | bytes 1572868
  103.3 3.5 %copy-start.19 = (bf16[1,256,2,512]{1,3,2,0:T(8,128)(2,1)}, bf16[1,256,2,512]{1,3,2,0:T(8,128)(2,1)S(1)}, u32[]{:S(2)}) copy-start(bf16[1,256,2,512]{1,3,2,0:T(8,128)(2,1)S(1)} %copy.192) | copy-start | bytes 1572868
  106.9 2.9 %copy-start.9 = (bf16[512,512]{1,0:T(8,128)(2,1)S(1)}, bf16[512,512]{1,0:T(8,128)(2,1)}, u32[]{:S(2)}) copy-start(bf16[512,512]{1,0:T(8,128)(2,1)} %param.18) | copy-start | bytes 1572868
  109.6 1.1 copy-start.22
  110.7 9.7 %copy-start.6 = (f32[16,16,2,512]{3,1,0,2:T(8,128)S(1)}, f32[16,16,2,512]{3,1,0,2:T(8,128)}, u32[]{:S(2)}) copy-start(f32[16,16,2,512]{3,1,0,2:T(8,128)} %copy.171) | copy-start | bytes 3145732
  122.8 3.5 %copy-start.8 = (f32[2,8,256,256]{2,3,1,0:T(8,128)S(1)}, f32[2,8,256,256]{2,3,1,0:T(8,128)}, u32[]{:S(2)}) copy-start(f32[2,8,256,256]{2,3,1,0:T(8,128)} %get-tuple-element.14) | copy-start | bytes 12582916
  122.8 3.6 %copy-start.20 = (bf16[1,256,2,512]{1,3,2,0:T(8,128)(2,1)S(1)}, bf16[1,256,2,512]{1,3,2,0:T(8,128)(2,1)}, u32[]{:S(2)}) copy-start(bf16[1,256,2,512]{1,3,2,0:T(8,128)(2,1)} %copy-done.19) | copy-start | bytes 1572868
  127.5 1.0 copy-start.17
  127.5 1.8 copy-start.15
  135.3 38.0 %copy-start.11 = (bf16[512,512]{1,0:T(8,128)(2,1)S(1)}, bf16[512,512]{1,0:T(8,128)(2,1)}, u32[]{:S(2)}) copy-start(bf16[512,512]{1,0:T(8,128)(2,1)} %param.15) | copy-start | bytes 1572868
  172.6 0.8 copy-start.4
  174.0 3.9 %copy-start.7 = (f32[2,8,256,256]{2,3,1,0:T(8,128)S(1)}, f32[2,8,256,256]{2,3,1,0:T(8,128)}, u32[]{:S(2)}) copy-start(f32[2,8,256,256]{2,3,1,0:T(8,128)} %get-tuple-element.12) | copy-start | bytes 12582916
  174.0 3.9 %copy-start.18 = (bf16[256,1,2,512]{0,3,2,1:T(8,128)(2,1)S(1)}, bf16[256,1,2,512]{0,3,2,1:T(8,128)(2,1)}, u32[]{:S(2)}) copy-start(bf16[256,1,2,512]{0,3,2,1:T(8,128)(2,1)} %copy.181) | copy-start | bytes 1572868
  178.8 1.0 copy-start.13
  178.8 2.6 %copy-start.12 = (bf16[256,1,2,512]{0,3,2,1:T(8,128)(2,1)S(1)}, bf16[256,1,2,512]{0,3,2,1:T(8,128)(2,1)}, u32[]{:S(2)}) copy-start(bf16[256,1,2,512]{0,3,2,1:T(8,128)(2,1)} %copy.183) | copy-start | bytes 1572868
  179.9 6.6 %copy-start.3 = (f32[16,16,1,2,512]{4,1,0,3,2:T(8,128)S(1)}, f32[16,16,1,2,512]{4,1,0,3,2:T(8,128)}, u32[]{:S(2)}) copy-start(f32[16,16,1,2,512]{4,1,0,3,2:T(8,128)} %copy-done.2) | copy-start | bytes 3145732
  186.5 3.0 %copy-start.5 = (bf16[16,16,1,2,512]{4,1,0,3,2:T(8,128)(2,1)S(1)}, bf16[16,16,1,2,512]{4,1,0,3,2:T(8,128)(2,1)}, u32[]{:S(2)}) copy-start(bf16[16,16,1,2,512]{4,1,0,3,2:T(8,128)(2,1)} %copy-done.4) | copy-start | bytes 1572868
  189.1 23.6 %copy-start.1 = (bf16[2048,512]{1,0:T(8,128)(2,1)S(1)}, bf16[2048,512]{1,0:T(8,128)(2,1)}, u32[]{:S(2)}) copy-start(bf16[2048,512]{1,0:T(8,128)(2,1)} %param.21) | copy-start | bytes 6291460
